TPU v7x, 256 devices: a whole 4x4x8 slice. The times are simulated.
256 devices in a mesh: row: 8 (over z), col: 32 (over x, y, core).
Axes of the slice: x: 4, y: 4, z: 8, core: 2. Of those that a mesh axis runs over, the one named last changes fastest.
Arguments:
- three_index: float32 [256, 512, 1024], P('col', None, 'row'), may hold values from -1.2 to 1.2
- occ_energy: float32 [256], replicated, may hold values from -2 to -0.5
- vir_energy: float32 [512], replicated, may hold values from 0.5 to 3
- block_mask: int32 [256, 8, 16], replicated, may hold values from 0 to 1, as said below
- pair_list: int32 [256, 4], P('col'), may hold values from -1 to 3, as said below
Outputs:
- response_density: float32 [256, 512, 1024], P('col', None, 'row')
- virtual_density: float32 [512, 512], replicated
Inputs may be any that keep to these rules, and one draw needn't show every extreme that they name: `block_mask`: each orbital keeps between 32 and 64 of its 128 blocks; some orbital keeps exactly 64. `pair_list`: in each row the live entries come first and are distinct, then -1; every orbital lists at least one partner class; some orbital lists 4.
All inputs are finite; a program needn't handle non-finite values.
Results may differ from a plain program's by a relative error of at most 0.0003.
Values sent between devices are 32-bit elements; how exact they have to be, the bound alone decides.
A program may use at most 128 MiB of HBM per device.

v0:
```python
import jax
import jax.numpy as jnp
from jax import lax
from jax.sharding import PartitionSpec as P

NVIR = 512
NAUX = 1024
BLOCK = 64
STEPS = 2
PAIRS_DEV = 4


def spread(block, axis, holder):
    block = jnp.where(lax.axis_index(axis) == holder, block, jnp.zeros_like(block))
    return lax.psum(block, axis)


def expand_mask(block_rows):
    widened = jnp.repeat(block_rows.astype(jnp.float32), BLOCK, axis=-2)
    return jnp.repeat(widened, BLOCK, axis=-1)


def pair_terms(own_rows, partner, energy_own, energy_partner, virtual):
    cross_term = lax.dot_general(
        own_rows,
        partner,
        (((1,), (1,)), ((), ())),
        precision=lax.Precision.HIGHEST,
        preferred_element_type=jnp.float32,
    )
    denominator = energy_own + energy_partner - virtual[:, None] - virtual[None, :]
    amplitude = cross_term / denominator
    weighted = 2.0 * amplitude - amplitude.T
    response = jnp.dot(
        weighted, partner, precision=lax.Precision.HIGHEST, preferred_element_type=jnp.float32
    )
    virt_density = lax.dot_general(
        weighted,
        amplitude,
        (((1,), (1,)), ((), ())),
        precision=lax.Precision.HIGHEST,
        preferred_element_type=jnp.float32,
    )
    return (response, virt_density)


def on_device(three_index, occ_energy, vir_energy, block_mask, pair_list):
    row_index = lax.axis_index("row")
    col_index = lax.axis_index("col")
    row_count = lax.axis_size("row")
    col_count = lax.axis_size("col")
    own_orbital = col_index * row_count + row_index
    gathered = lax.all_to_all(three_index, "row", split_axis=0, concat_axis=2, tiled=True)
    own_rows = gathered[0] * expand_mask(block_mask[own_orbital])
    panels = []
    for owner_step in range(STEPS):
        first_root = 2 * owner_step
        second_root = first_root + 1
        panels.append(spread(own_rows, "col", first_root))
        panels.append(spread(own_rows, "col", second_root))
    stacked = jnp.stack(panels)
    energy_own = occ_energy[own_orbital]
    response_sum = jnp.zeros((NVIR, NAUX), jnp.float32)
    density_sum = jnp.zeros((NVIR, NVIR), jnp.float32)
    for slot_index in range(PAIRS_DEV):
        listed = pair_list[row_index, slot_index]
        panel_index = jnp.maximum(listed, 0)
        partner = stacked[panel_index]
        energy_partner = occ_energy[panel_index * row_count + row_index]
        live = (listed >= 0).astype(jnp.float32)
        response, virt_density = pair_terms(
            own_rows, partner, energy_own, energy_partner, vir_energy
        )
        response = live * response
        virt_density = live * virt_density
        response_sum = response_sum + response
        density_sum = density_sum + virt_density
    returned = lax.all_to_all(response_sum[None], "row", split_axis=2, concat_axis=0, tiled=True)
    total = lax.psum(density_sum, ("row", "col"))
    return (returned, total / (row_count * col_count))


def solution(mesh):
    placed = (P("col", None, "row"), P(), P(), P(), P("col", None))
    return jax.shard_map(
        on_device,
        mesh=mesh,
        in_specs=placed,
        out_specs=(P("col", None, "row"), P()),
        check_vma=False,
    )
```

profile of v0, /device:TPU:2, one launch (start us, length us, event | category | flops | bytes accessed | tf_op | source)
XLA Modules:
  0.0 567.0 jit_solution(334607822717897980)
XLA Ops:
  7.2 2.9 copy.21
  10.1 8.5 %all-to-all-start = ((f32[8,512,128]{1,2,0:T(8,128)}), f32[8,512,128]{1,2,0:T(8,128)S(1)}, u32[]{:S(2)}, u32[]{:S(2)}) async-start(f32[8,512,128]{1,2,0:T(8,128)} %copy.21), calls=%async_computation | async-start | bytes 4194304 | tf_op jit(solution)/shard_map/all_to_all | solution.py:53
  19.1 50.7 %all-to-all-done = f32[8,512,128]{1,2,0:T(8,128)S(1)} async-done(((f32[8,512,128]{1,2,0:T(8,128)}), f32[8,512,128]{1,2,0:T(8,128)S(1)}, u32[]{:S(2)}, u32[]{:S(2)}) %all-to-all-start) | async-done | bytes 2097184 | tf_op jit(solution)/shard_map/all_to_all | solution.py:53
  69.8 3.9 select_bitcast_fusion
  74.4 0.7 constant_dynamic-slice_fusion.1
  80.2 0.7 fusion.49
  86.0 2.2 bitcast_multiply_fusion.1
  88.2 111.9 %all-reduce.6.cloned.1.call-done = (f32[1,512,1024]{1,2,0:T(8,128)}, f32[1,512,1024]{1,2,0:T(8,128)}, f32[1,512,1024]{1,2,0:T(8,128)}, f32[1,512,1024]{1,2,0:T(8,128)}) async-done(((f32[1,512,1024]{1,2,0:T(8,128)}, f32[1,512,1024]{1,2,0:T(8,128)}, f32[1,512,1024]{1,2,0:T(8,128)}, f32[1,512,1024]{1,2,0:T(8,128)}), (f32[1,512,1024]{1,2,0:T(8,128)}, f32[1,512,1024]{1,2,0:T(8,128)}, f32[1,512,1024]{1,2,0:T(8,128)}, ...) | async-done | bytes 8388624 | tf_op jit(solution)/shard_map/psum | solution.py:15
  200.2 1.9 constant_dynamic-update-slice_fusion.3
  202.6 1.4 copy-done.9
  204.2 1.4 copy-done.8
  205.8 3.5 fusion.2
  209.3 4.6 fusion.6
  213.9 4.9 fusion.10
  218.7 4.5 fusion.14
  223.3 2.7 copy.24
  225.9 1.3 copy.25
  227.3 1.3 copy.26
  228.6 1.3 copy.27
  229.9 9.2 %fusion.8 = f32[512,1024]{1,0:T(8,128)S(1)} fusion(f32[4,512,1024]{1,2,0:T(8,128)} %copy-done.2, s32[]{:T(128)} %bitcast.18, f32[512,512]{1,0:T(8,128)S(1)} %copy-done.5, f32[512]{0:T(512)S(1)} %get-tuple-element.11, f32[512]{0:T(512)S(1)} %copy-done.19, f32[512,512]{0,1:T(8,128)} %copy.25), kind=kOutput, calls=%fused_computation.9 | convolution fusion | flops 3222798336 | bytes 6300160 | tf_op jit(solution)/shard_map/dot_general | solution.py:34
  239.1 8.7 %fusion.4 = f32[512,1024]{1,0:T(8,128)S(1)} fusion(f32[4,512,1024]{1,2,0:T(8,128)} %copy-done.2, s32[]{:T(128)} %bitcast.23, f32[512,512]{1,0:T(8,128)S(1)} %copy-done.3, f32[512]{0:T(512)S(1)} %get-tuple-element.13, f32[512]{0:T(512)S(1)} %copy-done.19, f32[512,512]{0,1:T(8,128)S(1)} %copy-done.13), kind=kOutput, calls=%fused_computation.5 | convolution fusion | flops 3222798336 | bytes 6300160 | tf_op jit(solution)/shard_map/dot_general | solution.py:34
  247.9 7.2 %fusion = f32[512,1024]{1,0:T(8,128)S(1)} fusion(f32[4,512,1024]{1,2,0:T(8,128)S(1)} %bitcast.112, s32[]{:T(128)} %bitcast.28, f32[512,512]{1,0:T(8,128)S(1)} %fusion.2, f32[512]{0:T(512)S(1)} %get-tuple-element.12, f32[512]{0:T(512)S(1)} %copy-done.19, f32[512,512]{0,1:T(8,128)S(1)} %copy-done.11), kind=kOutput, calls=%fused_computation.1 | convolution fusion | flops 3222798336 | bytes 6299652 | tf_op jit(solution)/shard_map/dot_general | solution.py:34
  255.1 7.2 %add_bitcast_fusion = f32[1,512,1024]{2,1,0:T(8,128)S(1)} fusion(f32[512,1024]{1,0:T(8,128)S(1)} %fusion, f32[512,1024]{1,0:T(8,128)S(1)} %fusion.4, f32[512,1024]{1,0:T(8,128)S(1)} %fusion.8, f32[4,512,1024]{1,2,0:T(8,128)S(1)} %bitcast.112, s32[]{:T(128)} %bitcast.13, f32[]{:T(128)} %bitcast.27, f32[]{:T(128)} %bitcast.22, f32[]{:T(128)} %bitcast.17, ...), kind=kOutput, calls=%fused_computation.18 | convolution fusion | flops 3226468352 | bytes 12591124 | tf_op jit(solution)/shard_map/dot_general | solution.py:34
  262.3 3.7 copy.28
  266.0 7.0 %all-to-all-start.1 = ((f32[1,512,1024]{1,0,2:T(1,128)}), f32[1,512,1024]{1,0,2:T(1,128)S(1)}, u32[]{:S(2)}, u32[]{:S(2)}) async-start(f32[1,512,1024]{1,0,2:T(1,128)} %copy.28), calls=%async_computation.1 | async-start | bytes 4194304 | tf_op jit(solution)/shard_map/all_to_all | solution.py:78
  273.3 4.5 convolution_multiply_fusion.3
  277.8 2.5 fusion.28
  280.4 2.5 fusion.27
  282.9 3.5 fusion.26
  286.4 267.5 %all-reduce.4.cloned.1.call-done = f32[512,512]{1,0:T(8,128)} async-done(((f32[512,512]{1,0:T(8,128)}), f32[512,512]{1,0:T(8,128)}) %all-reduce.4.cloned.1.call-update) | async-done | bytes 1048592 | tf_op jit(solution)/shard_map/psum | solution.py:79
  553.9 2.3 broadcast_multiply_fusion
  556.2 3.6 copy.29
  (59 shorter events, 2.6 us)
Async XLA Ops:
  7.2 11.5 %copy-start = (s32[256,8,16]{0,2,1:T(8,128)S(1)}, s32[256,8,16]{0,2,1:T(8,128)}, u32[]{:S(2)}) copy-start(s32[256,8,16]{0,2,1:T(8,128)} %param.8) | copy-start | bytes 393220
  10.1 59.7 %all-to-all-start = ((f32[8,512,128]{1,2,0:T(8,128)}), f32[8,512,128]{1,2,0:T(8,128)S(1)}, u32[]{:S(2)}, u32[]{:S(2)}) async-start(f32[8,512,128]{1,2,0:T(8,128)} %copy.21), calls=%async_computation | async-start | bytes 4194304 | tf_op jit(solution)/shard_map/all_to_all | solution.py:53
  18.6 181.6 %all-reduce.6.cloned.1.call-start = ((), (), s32[]{:S(2)}) async-start(), calls=%async_computation.3 | async-start | bytes 16777216 | tf_op jit(solution)/shard_map/psum | solution.py:15
  69.8 4.0 copy-start.1
  73.7 0.7 copy-start.18
  73.7 6.4 %copy-start.17 = (f32[256]{0:T(256)S(1)}, f32[256]{0:T(256)}, u32[]{:S(2)}) copy-start(f32[256]{0:T(256)} %param.6) | copy-start | bytes 3076
  73.7 12.0 %copy-start.19 = (f32[512]{0:T(512)S(1)}, f32[512]{0:T(512)}, u32[]{:S(2)}) copy-start(f32[512]{0:T(512)} %param.7) | copy-start | bytes 6148
  200.2 2.2 copy-start.10
  202.4 1.6 copy-start.9
  204.0 1.6 copy-start.8
  205.8 13.0 %copy-start.2 = (f32[4,512,1024]{1,2,0:T(8,128)}, f32[4,512,1024]{1,2,0:T(8,128)S(1)}, u32[]{:S(2)}) copy-start(f32[4,512,1024]{1,2,0:T(8,128)S(1)} %constant_dynamic-update-slice_fusion) | copy-start | bytes 25165828
  223.2 2.7 copy-start.5
  223.2 4.0 copy-start.3
  229.9 9.2 %copy-start.13 = (f32[512,512]{0,1:T(8,128)S(1)}, f32[512,512]{0,1:T(8,128)}, u32[]{:S(2)}) copy-start(f32[512,512]{0,1:T(8,128)} %copy.26) | copy-start | bytes 3145732
  229.9 17.9 %slice-start = ((s8[8388608]{0:T(1024)(128)(4,1)}), s8[4194304]{0:T(1024)(128)(4,1)S(1)}, s32[]{:S(2)}) async-start(s8[8388608]{0:T(1024)(128)(4,1)} %bitcast.111), calls=%async_computation.4 | async-start | bytes 8388608
  239.1 8.7 %slice-start.1 = ((s8[8388608]{0:T(1024)(128)(4,1)}), s8[4194304]{0:T(1024)(128)(4,1)S(1)}, s32[]{:S(2)}) async-start(s8[8388608]{0:T(1024)(128)(4,1)} %bitcast.111), calls=%async_computation.5 | async-start | bytes 8388608
  239.1 8.7 %copy-start.11 = (f32[512,512]{0,1:T(8,128)S(1)}, f32[512,512]{0,1:T(8,128)}, u32[]{:S(2)}) copy-start(f32[512,512]{0,1:T(8,128)} %copy.27) | copy-start | bytes 3145732
  247.9 7.2 %copy-start.7 = (f32[512,512]{1,0:T(8,128)S(1)}, f32[512,512]{1,0:T(8,128)}, u32[]{:S(2)}) copy-start(f32[512,512]{1,0:T(8,128)} %fusion.14) | copy-start | bytes 3145732
  247.9 7.2 %copy-start.16 = (f32[512,512]{0,1:T(8,128)S(1)}, f32[512,512]{0,1:T(8,128)}, u32[]{:S(2)}) copy-start(f32[512,512]{0,1:T(8,128)} %copy.24) | copy-start | bytes 3145732
  266.0 290.2 %all-to-all-start.1 = ((f32[1,512,1024]{1,0,2:T(1,128)}), f32[1,512,1024]{1,0,2:T(1,128)S(1)}, u32[]{:S(2)}, u32[]{:S(2)}) async-start(f32[1,512,1024]{1,0,2:T(1,128)} %copy.28), calls=%async_computation.1 | async-start | bytes 4194304 | tf_op jit(solution)/shard_map/all_to_all | solution.py:78
  273.0 280.9 %all-reduce.4.cloned.1.call-start = ((), (), s32[]{:S(2)}) async-start(), calls=%async_computation.2 | async-start | bytes 2097152 | tf_op jit(solution)/shard_map/psum | solution.py:79
  273.3 4.5 copy-start.6
  273.3 4.5 copy-start.15
  277.8 2.5 copy-start.4
  277.8 2.5 copy-start.14
  280.3 2.5 copy-start.12
Sparse Core Ops, SparseCore 0:
  73.9 126.2 all-reduce.5
  286.5 267.3 all-reduce.3
where the time goes:
time: 576 us; the launch traced here: 567 us
  waiting for transfers between devices  430 us (75%)
  matrix products  62.6 us (11%)
  local copies, waits for them, and re-layouts  25.2 us (4%)
  between operations  24.9 us (4%)
  starting transfers between devices  15.8 us (3%)
  other arithmetic  8.42 us (1%)
    psum x1, waiting for transfers between devices, on_device(): total = lax.psum(density_sum, ('row', 'col'))  267 us
    psum x1, waiting for transfers between devices, spread(): return lax.psum(block, axis)  112 us
    all_to_all x1, waiting for transfers between devices, on_device(): lax.all_to_all(three_index, 'row', split_axis=0, concat_axis=2, tiled=True)  50.7 us
    dot_general x4, matrix products, pair_terms(): jnp.dot(weighted, partner, precision=lax.Precision.HIGHEST, preferred_ele...  32.2 us
    dot_general x4, matrix products, pair_terms(): lax.dot_general(own_rows, partner, (((1,), (1,)), ((), ())), precision=la...  17.5 us
    dot_general x4, matrix products, pair_terms(): lax.dot_general(weighted, amplitude, (((1,), (1,)), ((), ())), precision=...  12.9 us
  transfers between devices with their start and end apart: 4, of which 3 were waited for; matrix products, arithmetic and copies ran while one was open for 3% of the time, Pallas kernels for 0%

commit v1 on v0

--- a/solution.py
+++ b/solution.py
@@ -76,7 +76,9 @@
         response_sum = response_sum + response
         density_sum = density_sum + virt_density
     returned = lax.all_to_all(response_sum[None], "row", split_axis=2, concat_axis=0, tiled=True)
-    total = lax.psum(density_sum, ("row", "col"))
+    total = density_sum
+    for mesh_axis in ("col", "row"):
+        total = lax.psum(total, mesh_axis)
     return (returned, total / (row_count * col_count))
 
 

time: 576 us -> 503 us (0.87)
  waiting for transfers between devices: 430 us -> 357 us
    psum x1 -> x2, waiting for transfers between devices: 267 us -> 194 us  [on_device(): total = lax.psum(total, mesh_axis)]
  transfers between devices with their start and end apart: 4 -> 5, of which waited for: 3 -> 4; matrix products, arithmetic and copies ran while one was open for 3% -> 4% of each run, Pallas kernels for 0% -> 0%
where the time goes in v1:
time: 503 us; the launch traced here: 493 us
  waiting for transfers between devices  357 us (71%)
  matrix products  62.6 us (12%)
  local copies, waits for them, and re-layouts  25.2 us (5%)
  between operations  24.6 us (5%)
  starting transfers between devices  15.8 us (3%)
  other arithmetic  8.42 us (2%)
    psum x2, waiting for transfers between devices, on_device(): total = lax.psum(total, mesh_axis)  194 us
    psum x1, waiting for transfers between devices, spread(): return lax.psum(block, axis)  112 us
    all_to_all x1, waiting for transfers between devices, on_device(): lax.all_to_all(three_index, 'row', split_axis=0, concat_axis=2, tiled=True)  50.7 us
    dot_general x4, matrix products, pair_terms(): jnp.dot(weighted, partner, precision=lax.Precision.HIGHEST, preferred_ele...  32.2 us
    dot_general x4, matrix products, pair_terms(): lax.dot_general(own_rows, partner, (((1,), (1,)), ((), ())), precision=la...  17.5 us
    dot_general x4, matrix products, pair_terms(): lax.dot_general(weighted, amplitude, (((1,), (1,)), ((), ())), precision=...  12.9 us
  transfers between devices with their start and end apart: 5, of which 4 were waited for; matrix products, arithmetic and copies ran while one was open for 4% of the time, Pallas kernels for 0%

profile of v1, /device:TPU:2, one launch (start us, length us, event | category | flops | bytes accessed | tf_op | source)
XLA Modules:
  0.0 493.4 jit_solution(7626510109737564094)
XLA Ops:
  7.2 2.9 copy.21
  10.1 8.5 %all-to-all-start = ((f32[8,512,128]{1,2,0:T(8,128)}), f32[8,512,128]{1,2,0:T(8,128)S(1)}, u32[]{:S(2)}, u32[]{:S(2)}) async-start(f32[8,512,128]{1,2,0:T(8,128)} %copy.21), calls=%async_computation | async-start | bytes 4194304 | tf_op jit(solution)/shard_map/all_to_all | solution.py:53
  19.1 50.7 %all-to-all-done = f32[8,512,128]{1,2,0:T(8,128)S(1)} async-done(((f32[8,512,128]{1,2,0:T(8,128)}), f32[8,512,128]{1,2,0:T(8,128)S(1)}, u32[]{:S(2)}, u32[]{:S(2)}) %all-to-all-start) | async-done | bytes 2097184 | tf_op jit(solution)/shard_map/all_to_all | solution.py:53
  69.8 3.9 select_bitcast_fusion
  80.2 0.7 fusion.49
  86.0 2.2 bitcast_multiply_fusion.1
  88.2 111.9 %all-reduce.9.cloned.1.call-done = (f32[1,512,1024]{1,2,0:T(8,128)}, f32[1,512,1024]{1,2,0:T(8,128)}, f32[1,512,1024]{1,2,0:T(8,128)}, f32[1,512,1024]{1,2,0:T(8,128)}) async-done(((f32[1,512,1024]{1,2,0:T(8,128)}, f32[1,512,1024]{1,2,0:T(8,128)}, f32[1,512,1024]{1,2,0:T(8,128)}, f32[1,512,1024]{1,2,0:T(8,128)}), (f32[1,512,1024]{1,2,0:T(8,128)}, f32[1,512,1024]{1,2,0:T(8,128)}, f32[1,512,1024]{1,2,0:T(8,128)}, ...) | async-done | bytes 8388624 | tf_op jit(solution)/shard_map/psum | solution.py:15
  200.2 1.9 constant_dynamic-update-slice_fusion.3
  202.6 1.4 copy-done.9
  204.2 1.4 copy-done.8
  205.8 3.5 fusion.2
  209.3 4.6 fusion.6
  213.9 4.9 fusion.10
  218.7 4.5 fusion.14
  223.3 2.7 copy.24
  225.9 1.3 copy.25
  227.3 1.3 copy.26
  228.6 1.3 copy.27
  229.9 9.2 %fusion.8 = f32[512,1024]{1,0:T(8,128)S(1)} fusion(f32[4,512,1024]{1,2,0:T(8,128)} %copy-done.2, s32[]{:T(128)} %bitcast.18, f32[512,512]{1,0:T(8,128)S(1)} %copy-done.5, f32[512]{0:T(512)S(1)} %get-tuple-element.11, f32[512]{0:T(512)S(1)} %copy-done.19, f32[512,512]{0,1:T(8,128)} %copy.25), kind=kOutput, calls=%fused_computation.9 | convolution fusion | flops 3222798336 | bytes 6300160 | tf_op jit(solution)/shard_map/dot_general | solution.py:34
  239.1 8.7 %fusion.4 = f32[512,1024]{1,0:T(8,128)S(1)} fusion(f32[4,512,1024]{1,2,0:T(8,128)} %copy-done.2, s32[]{:T(128)} %bitcast.23, f32[512,512]{1,0:T(8,128)S(1)} %copy-done.3, f32[512]{0:T(512)S(1)} %get-tuple-element.13, f32[512]{0:T(512)S(1)} %copy-done.19, f32[512,512]{0,1:T(8,128)S(1)} %copy-done.13), kind=kOutput, calls=%fused_computation.5 | convolution fusion | flops 3222798336 | bytes 6300160 | tf_op jit(solution)/shard_map/dot_general | solution.py:34
  247.9 7.2 %fusion = f32[512,1024]{1,0:T(8,128)S(1)} fusion(f32[4,512,1024]{1,2,0:T(8,128)S(1)} %bitcast.112, s32[]{:T(128)} %bitcast.28, f32[512,512]{1,0:T(8,128)S(1)} %fusion.2, f32[512]{0:T(512)S(1)} %get-tuple-element.12, f32[512]{0:T(512)S(1)} %copy-done.19, f32[512,512]{0,1:T(8,128)S(1)} %copy-done.11), kind=kOutput, calls=%fused_computation.1 | convolution fusion | flops 3222798336 | bytes 6299652 | tf_op jit(solution)/shard_map/dot_general | solution.py:34
  255.1 7.2 %add_bitcast_fusion = f32[1,512,1024]{2,1,0:T(8,128)S(1)} fusion(f32[512,1024]{1,0:T(8,128)S(1)} %fusion, f32[512,1024]{1,0:T(8,128)S(1)} %fusion.4, f32[512,1024]{1,0:T(8,128)S(1)} %fusion.8, f32[4,512,1024]{1,2,0:T(8,128)S(1)} %bitcast.112, s32[]{:T(128)} %bitcast.13, f32[]{:T(128)} %bitcast.27, f32[]{:T(128)} %bitcast.22, f32[]{:T(128)} %bitcast.17, ...), kind=kOutput, calls=%fused_computation.18 | convolution fusion | flops 3226468352 | bytes 12591124 | tf_op jit(solution)/shard_map/dot_general | solution.py:34
  262.3 3.7 copy.28
  266.0 7.0 %all-to-all-start.1 = ((f32[1,512,1024]{1,0,2:T(1,128)}), f32[1,512,1024]{1,0,2:T(1,128)S(1)}, u32[]{:S(2)}, u32[]{:S(2)}) async-start(f32[1,512,1024]{1,0,2:T(1,128)} %copy.28), calls=%async_computation.1 | async-start | bytes 4194304 | tf_op jit(solution)/shard_map/all_to_all | solution.py:78
  273.3 4.5 convolution_multiply_fusion.3
  277.8 2.5 fusion.28
  280.4 2.5 fusion.27
  282.9 3.5 fusion.26
  286.4 115.4 %all-reduce.5.cloned.1.call-done = f32[512,512]{1,0:T(8,128)} async-done(((f32[512,512]{1,0:T(8,128)}), f32[512,512]{1,0:T(8,128)}) %all-reduce.5.cloned.1.call-update) | async-done | bytes 1048592 | tf_op jit(solution)/shard_map/psum | solution.py:81
  401.9 78.7 %all-reduce.7.cloned.1.call-done = f32[512,512]{1,0:T(8,128)} async-done(((f32[512,512]{1,0:T(8,128)}), f32[512,512]{1,0:T(8,128)}) %all-reduce.7.cloned.1.call-update) | async-done | bytes 1048592 | tf_op jit(solution)/shard_map/psum | solution.py:81
  480.6 2.3 broadcast_multiply_fusion
  482.9 3.6 copy.29
  (62 shorter events, 3.3 us)
Async XLA Ops:
  7.2 11.5 %copy-start = (s32[256,8,16]{0,2,1:T(8,128)S(1)}, s32[256,8,16]{0,2,1:T(8,128)}, u32[]{:S(2)}) copy-start(s32[256,8,16]{0,2,1:T(8,128)} %param.8) | copy-start | bytes 393220
  10.1 59.7 %all-to-all-start = ((f32[8,512,128]{1,2,0:T(8,128)}), f32[8,512,128]{1,2,0:T(8,128)S(1)}, u32[]{:S(2)}, u32[]{:S(2)}) async-start(f32[8,512,128]{1,2,0:T(8,128)} %copy.21), calls=%async_computation | async-start | bytes 4194304 | tf_op jit(solution)/shard_map/all_to_all | solution.py:53
  18.6 181.6 %all-reduce.9.cloned.1.call-start = ((), (), s32[]{:S(2)}) async-start(), calls=%async_computation.4 | async-start | bytes 16777216 | tf_op jit(solution)/shard_map/psum | solution.py:15
  69.8 4.0 copy-start.1
  73.7 0.7 copy-start.18
  73.7 6.4 %copy-start.17 = (f32[256]{0:T(256)S(1)}, f32[256]{0:T(256)}, u32[]{:S(2)}) copy-start(f32[256]{0:T(256)} %param.6) | copy-start | bytes 3076
  73.7 12.0 %copy-start.19 = (f32[512]{0:T(512)S(1)}, f32[512]{0:T(512)}, u32[]{:S(2)}) copy-start(f32[512]{0:T(512)} %param.7) | copy-start | bytes 6148
  200.2 2.2 copy-start.10
  202.4 1.6 copy-start.9
  204.0 1.6 copy-start.8
  205.8 13.0 %copy-start.2 = (f32[4,512,1024]{1,2,0:T(8,128)}, f32[4,512,1024]{1,2,0:T(8,128)S(1)}, u32[]{:S(2)}) copy-start(f32[4,512,1024]{1,2,0:T(8,128)S(1)} %constant_dynamic-update-slice_fusion) | copy-start | bytes 25165828
  223.2 2.7 copy-start.5
  223.2 4.0 copy-start.3
  229.9 9.2 %copy-start.13 = (f32[512,512]{0,1:T(8,128)S(1)}, f32[512,512]{0,1:T(8,128)}, u32[]{:S(2)}) copy-start(f32[512,512]{0,1:T(8,128)} %copy.26) | copy-start | bytes 3145732
  229.9 17.9 %slice-start = ((s8[8388608]{0:T(1024)(128)(4,1)}), s8[4194304]{0:T(1024)(128)(4,1)S(1)}, s32[]{:S(2)}) async-start(s8[8388608]{0:T(1024)(128)(4,1)} %bitcast.111), calls=%async_computation.5 | async-start | bytes 8388608
  239.1 8.7 %slice-start.1 = ((s8[8388608]{0:T(1024)(128)(4,1)}), s8[4194304]{0:T(1024)(128)(4,1)S(1)}, s32[]{:S(2)}) async-start(s8[8388608]{0:T(1024)(128)(4,1)} %bitcast.111), calls=%async_computation.6 | async-start | bytes 8388608
  239.1 8.7 %copy-start.11 = (f32[512,512]{0,1:T(8,128)S(1)}, f32[512,512]{0,1:T(8,128)}, u32[]{:S(2)}) copy-start(f32[512,512]{0,1:T(8,128)} %copy.27) | copy-start | bytes 3145732
  247.9 7.2 %copy-start.7 = (f32[512,512]{1,0:T(8,128)S(1)}, f32[512,512]{1,0:T(8,128)}, u32[]{:S(2)}) copy-start(f32[512,512]{1,0:T(8,128)} %fusion.14) | copy-start | bytes 3145732
  247.9 7.2 %copy-start.16 = (f32[512,512]{0,1:T(8,128)S(1)}, f32[512,512]{0,1:T(8,128)}, u32[]{:S(2)}) copy-start(f32[512,512]{0,1:T(8,128)} %copy.24) | copy-start | bytes 3145732
  266.0 216.9 %all-to-all-start.1 = ((f32[1,512,1024]{1,0,2:T(1,128)}), f32[1,512,1024]{1,0,2:T(1,128)S(1)}, u32[]{:S(2)}, u32[]{:S(2)}) async-start(f32[1,512,1024]{1,0,2:T(1,128)} %copy.28), calls=%async_computation.1 | async-start | bytes 4194304 | tf_op jit(solution)/shard_map/all_to_all | solution.py:78
  273.0 128.9 %all-reduce.5.cloned.1.call-start = ((), (), s32[]{:S(2)}) async-start(), calls=%async_computation.2 | async-start | bytes 2097152 | tf_op jit(solution)/shard_map/psum | solution.py:81
  273.3 4.5 copy-start.6
  273.3 4.5 copy-start.15
  277.8 2.5 copy-start.4
  277.8 2.5 copy-start.14
  280.3 2.5 copy-start.12
  286.4 194.2 %all-reduce.7.cloned.1.call-start = ((), (), s32[]{:S(2)}) async-start(), calls=%async_computation.3 | async-start | bytes 2097152 | tf_op jit(solution)/shard_map/psum | solution.py:81
Sparse Core Ops, SparseCore 0:
  73.9 126.2 all-reduce.8
  286.5 115.3 all-reduce.4
  404.2 76.3 all-reduce.6
